TPU v7x, 256 devices: a whole 4x4x8 slice. The times are simulated.
256 devices in a mesh: dp: 8 (over x, core), space: 32 (over y, z).
Axes of the slice: x: 4, y: 4, z: 8, core: 2. Of those that a mesh axis runs over, the one named last changes fastest.
Arguments:
- features: bfloat16 [8, 262144, 128], P('dp', 'space'), may hold values from -6 to 6
- child_parent: int32 [8, 262144], P('dp', 'space'), may hold values from 0 to 65535, as said below
- child_code: int32 [8, 262144], P('dp', 'space'), may hold values from 0 to 7
- weight: bfloat16 [8, 128, 128], replicated, may hold values from -0.25 to 0.25
- out_grad: bfloat16 [8, 65536, 128], P('dp', 'space'), may hold values from -6 to 6
Outputs:
- parent_out: bfloat16 [8, 65536, 128], P('dp', 'space')
- feature_grad: bfloat16 [8, 262144, 128], P('dp', 'space')
- weight_grad: float32 [8, 128, 128], replicated
Inputs may be any that keep to these rules, and one draw needn't show every extreme that they name: Within one window, child_parent is nondecreasing along the 8192 rows of one device of space. Parent p lies on device p // 2048 of space; at most 512 rows of one device have their parent on one device, and on every device some device receives exactly 512. No two fine octants of a window share both parent and child_code.
All inputs are finite; a program needn't handle non-finite values.
Results may differ from a plain program's by a relative error of at most 0.001.
Values may be sent and summed in bfloat16 or wider, within the bound.
A program may use at most 128 MiB of HBM per device.

v0:
```python
import jax
import jax.numpy as jnp
from jax import lax
from jax.sharding import PartitionSpec as P


def gather_blocks(rows, starts, capacity):
    extended = jnp.concatenate([rows, jnp.zeros((capacity,) + rows.shape[1:], rows.dtype)], axis=0)

    def window(offset):
        return lax.dynamic_slice_in_dim(extended, offset, capacity, 0)

    return jax.vmap(window)(starts)


def spread_blocks(blocks, starts, row_count):
    capacity = blocks.shape[1]
    channels = blocks.shape[2]
    canvas = jnp.zeros((row_count + capacity, channels), blocks.dtype)
    numbers = lax.ScatterDimensionNumbers(
        update_window_dims=(1, 2), inserted_window_dims=(), scatter_dims_to_operand_dims=(0,)
    )
    placed = lax.scatter_add(canvas, starts[:, None], blocks, numbers)
    return placed[:row_count]


def per_device(features, child_parent, child_code, weight, out_grad):
    fine_rows = features[0]
    parents = child_parent[0]
    child_kinds = child_code[0]
    cotangent = out_grad[0]
    row_count = fine_rows.shape[0]
    par_rows = cotangent.shape[0]
    kinds_total = weight.shape[0]
    chan_in = weight.shape[1]
    chan_out = weight.shape[2]
    space_size = lax.axis_size("space")
    capacity = 2 * row_count // space_size
    owners = parents // par_rows
    local_slot = (parents - owners * par_rows) * kinds_total + child_kinds
    counts = jnp.sum((owners[:, None] == jnp.arange(space_size)[None, :]).astype(jnp.int32), axis=0)
    starts = jnp.cumsum(counts) - counts
    slot_lane = jnp.arange(capacity)
    live_mask = slot_lane[None, :] < counts[:, None]
    marker = kinds_total * par_rows
    slot_blocks = gather_blocks(local_slot[:, None], starts, capacity)[:, :, 0]
    send_slots = jnp.where(live_mask, slot_blocks, marker)
    block_rows = min(512, row_count)
    block_count = row_count // block_rows
    kind_onehot = (child_kinds[:, None] == jnp.arange(kinds_total)[None, :]).astype(jnp.bfloat16)
    weight_cat = jnp.transpose(weight, (1, 0, 2)).reshape(chan_in, kinds_total * chan_out)
    weight_back = jnp.transpose(weight, (2, 0, 1)).reshape(chan_out, kinds_total * chan_in)
    rows_blocked = fine_rows.reshape(block_count, block_rows, chan_in)
    onehot_blocked = kind_onehot.reshape(block_count, block_rows, kinds_total)

    def forward_block(packed):
        rows, onehot = packed
        widened = jnp.dot(rows, weight_cat, preferred_element_type=jnp.float32).reshape(
            block_rows, kinds_total, chan_out
        )
        return jnp.sum(widened * onehot.astype(jnp.float32)[:, :, None], axis=1)

    products = lax.map(forward_block, (rows_blocked, onehot_blocked)).reshape(row_count, chan_out)
    part_blocks = gather_blocks(products, starts, capacity)
    send_parts = jnp.where(live_mask[:, :, None], part_blocks, 0.0)
    recv_parts, recv_slots = (
        lax.all_to_all(send_parts, "space", split_axis=0, concat_axis=0, tiled=True),
        lax.all_to_all(send_slots, "space", split_axis=0, concat_axis=0, tiled=True),
    )
    recv_parent = recv_slots // kinds_total
    summed = (
        jnp.zeros((par_rows, chan_out), jnp.float32)
        .at[recv_parent.reshape(-1)]
        .add(recv_parts.reshape(-1, chan_out), mode="drop")
    )
    result = summed.astype(jnp.bfloat16)
    back_rows = jnp.take(cotangent, recv_parent, axis=0, mode="fill", fill_value=0)
    returned = lax.all_to_all(back_rows, "space", split_axis=0, concat_axis=0, tiled=True)
    child_cot = spread_blocks(returned, starts, row_count)
    cot_blocked = child_cot.reshape(block_count, block_rows, chan_out)

    def backward_block(carry, packed):
        rows, onehot, cot = packed
        widened = jnp.dot(cot, weight_back, preferred_element_type=jnp.float32).reshape(
            block_rows, kinds_total, chan_in
        )
        grads = jnp.sum(widened * onehot.astype(jnp.float32)[:, :, None], axis=1).astype(
            jnp.bfloat16
        )
        placed = (rows[:, None, :] * onehot[:, :, None]).reshape(block_rows, kinds_total * chan_in)
        carry = carry + lax.dot_general(
            placed, cot, (((0,), (0,)), ((), ())), preferred_element_type=jnp.float32
        )
        return (carry, grads)

    start_term = jnp.zeros((kinds_total * chan_in, chan_out), jnp.float32)
    weight_term, grad_blocks = lax.scan(
        backward_block, start_term, (rows_blocked, onehot_blocked, cot_blocked)
    )
    feature_grad = grad_blocks.reshape(row_count, chan_in)
    summed_terms = lax.psum(weight_term, ("dp", "space"))
    total_rows = row_count * space_size * lax.axis_size("dp")
    weight_grad = (summed_terms / jnp.sqrt(jnp.float32(total_rows))).reshape(
        kinds_total, chan_in, chan_out
    )
    return (result[None], feature_grad[None], weight_grad)


def solution(mesh):
    placed = (
        P("dp", "space", None),
        P("dp", "space"),
        P("dp", "space"),
        P(),
        P("dp", "space", None),
    )
    return jax.shard_map(
        per_device,
        mesh=mesh,
        in_specs=placed,
        out_specs=(P("dp", "space", None), P("dp", "space", None), P()),
        check_vma=False,
    )
```

profile of v0, /device:TPU:2, one launch (start us, length us, event | category | flops | bytes accessed | tf_op | source)
XLA Modules:
  0.0 933.6 jit_solution(17775273788267957217)
XLA Ops:
  9.6 42.1 %while.32 = (s32[]{:T(128)}, s32[8704,1]{0,1:T(1,128)S(1)}, s32[32,2]{0,1:T(2,128)S(1)}, s32[32,512,1]{1,2,0:T(1,128)S(1)}) while((s32[]{:T(128)}, s32[8704,1]{0,1:T(1,128)S(1)}, s32[32,2]{0,1:T(2,128)S(1)}, s32[32,512,1]{1,2,0:T(1,128)S(1)}) %tuple.98), condition=%wide.while_cond.clone, body=%wide.while_body.sunk.clone | while | flops 2 | bytes 4193 | solution.py:11
  52.4 11.5 %all-to-all-start = ((s32[32,1,512]{2,1,0:T(1,128)}), s32[32,1,512]{2,1,0:T(1,128)S(1)}, u32[]{:S(2)}, u32[]{:S(2)}) async-start(s32[32,1,512]{2,1,0:T(1,128)} %compare_select_fusion.2), calls=%async_computation | async-start | bytes 131072 | tf_op jit(solution)/shard_map/all_to_all | solution.py:68
  67.1 37.0 %while.31 = (s32[]{:T(128)}, f32[16,512,128]{2,1,0:T(8,128)}, bf16[16,512,128]{2,1,0:T(8,128)(2,1)}, bf16[128,1024]{0,1:T(8,128)(2,1)S(1)}, bf16[16,512,8]{1,2,0:T(8,128)(2,1)S(1)}) while((s32[]{:T(128)}, f32[16,512,128]{2,1,0:T(8,128)}, bf16[16,512,128]{2,1,0:T(8,128)(2,1)}, bf16[128,1024]{0,1:T(8,128)(2,1)S(1)}, ...), condition=%wide.region_4.5_spmd.clone, body=%wide.region_2.4_spmd.sunk.clone | while | flops 135204864 | bytes 1220689 | solution.py:63
  104.5 57.4 %gather_fusion = bf16[16384,128]{1,0:T(8,128)(2,1)} fusion(bf16[2048,128]{1,0:T(8,128)(2,1)S(1)} %bitcast.167, s32[16384]{0:T(1024)S(1)} %broadcast_clamp_fusion), kind=kCustom, calls=%fused_computation | custom fusion | bytes 8454144 | tf_op jit(solution)/shard_map/jit(_take)/gather | solution.py:77
  161.9 7.7 broadcast_select_fusion.1
  169.6 9.9 %all-to-all-start.2 = ((bf16[32,512,128]{2,1,0:T(8,128)(2,1)}), bf16[32,512,128]{2,1,0:T(8,128)(2,1)}, u32[]{:S(2)}, u32[]{:S(2)}) async-start(bf16[32,512,128]{2,1,0:T(8,128)(2,1)} %broadcast_select_fusion.1), calls=%async_computation.2 | async-start | bytes 8388608 | tf_op jit(solution)/shard_map/all_to_all | solution.py:78
  179.6 3.8 concatenate.12
  183.4 93.2 %while.33 = (s32[]{:T(128)}, f32[8704,128]{1,0:T(8,128)}, s32[32,2]{0,1:T(2,128)S(1)}, f32[32,512,128]{2,1,0:T(8,128)}) while((s32[]{:T(128)}, f32[8704,128]{1,0:T(8,128)}, s32[32,2]{0,1:T(2,128)S(1)}, f32[32,512,128]{2,1,0:T(8,128)}) %tuple.121), condition=%wide.while_cond.1.clone, body=%wide.while_body.1.sunk.clone | while | flops 2 | bytes 524893 | solution.py:11
  184.0 2.3 bitcast_dynamic-update-slice_fusion.14
  187.0 2.3 bitcast_dynamic-update-slice_fusion.14
  189.9 2.3 bitcast_dynamic-update-slice_fusion.14
  192.8 2.3 bitcast_dynamic-update-slice_fusion.14
  195.7 2.3 bitcast_dynamic-update-slice_fusion.14
  198.6 2.3 bitcast_dynamic-update-slice_fusion.14
  201.5 2.3 bitcast_dynamic-update-slice_fusion.14
  204.4 2.3 bitcast_dynamic-update-slice_fusion.14
  207.3 2.3 bitcast_dynamic-update-slice_fusion.14
  210.3 2.3 bitcast_dynamic-update-slice_fusion.14
  213.2 2.3 bitcast_dynamic-update-slice_fusion.14
  216.1 2.3 bitcast_dynamic-update-slice_fusion.14
  219.0 2.3 bitcast_dynamic-update-slice_fusion.14
  221.9 2.3 bitcast_dynamic-update-slice_fusion.14
  224.8 2.3 bitcast_dynamic-update-slice_fusion.14
  227.7 2.3 bitcast_dynamic-update-slice_fusion.14
  230.6 2.3 bitcast_dynamic-update-slice_fusion.14
  233.5 2.3 bitcast_dynamic-update-slice_fusion.14
  236.4 2.3 bitcast_dynamic-update-slice_fusion.14
  239.4 2.3 bitcast_dynamic-update-slice_fusion.14
  242.3 2.3 bitcast_dynamic-update-slice_fusion.14
  245.2 2.3 bitcast_dynamic-update-slice_fusion.14
  248.1 2.3 bitcast_dynamic-update-slice_fusion.14
  251.0 2.3 bitcast_dynamic-update-slice_fusion.14
  253.9 2.3 bitcast_dynamic-update-slice_fusion.14
  256.8 2.3 bitcast_dynamic-update-slice_fusion.14
  259.7 2.3 bitcast_dynamic-update-slice_fusion.14
  262.6 2.3 bitcast_dynamic-update-slice_fusion.14
  265.5 2.3 bitcast_dynamic-update-slice_fusion.14
  268.4 2.3 bitcast_dynamic-update-slice_fusion.14
  271.4 2.3 bitcast_dynamic-update-slice_fusion.14
  274.3 2.3 bitcast_dynamic-update-slice_fusion.14
  276.6 9.9 %broadcast_select_fusion = f32[32,512,128]{2,1,0:T(8,128)} fusion(f32[32,512,128]{2,1,0:T(8,128)} %get-tuple-element.86, pred[32,512]{1,0:T(8,128)(4,1)S(1)} %iota_compare_fusion.2), kind=kLoop, calls=%fused_computation.28 | loop fusion | flops 2097152 | bytes 16793600 | tf_op jit(solution)/shard_map/jit(_where)/select_n | solution.py:65
  286.5 10.0 %all-to-all-start.1 = ((f32[32,512,128]{2,1,0:T(8,128)}), f32[32,512,128]{2,1,0:T(8,128)}, u32[]{:S(2)}, u32[]{:S(2)}) async-start(f32[32,512,128]{2,1,0:T(8,128)} %broadcast_select_fusion), calls=%async_computation.1 | async-start | bytes 16777216 | tf_op jit(solution)/shard_map/all_to_all | solution.py:67
  296.9 177.2 %while.34 = (s32[]{:T(128)}, bf16[8704,128]{1,0:T(8,128)(2,1)S(1)}, s32[32]{0:T(128)S(1)}, bf16[32,512,128]{2,1,0:T(8,128)(2,1)}, s32[2]{0:T(128)S(1)}, /*index=5*/s32[1]{0:T(128)}) while((s32[]{:T(128)}, bf16[8704,128]{1,0:T(8,128)(2,1)S(1)}, s32[32]{0:T(128)S(1)}, bf16[32,512,128]{2,1,0:T(8,128)(2,1)}, s32[2]{0:T(128)S(1)}, ...), condition=%wide.while_cond.2.clone, body=%wide.while_body.2.sunk.clone | while | flops 327691 | bytes 655479 | solution.py:23
  299.0 2.3 add_select_fusion.5
  304.5 2.3 add_select_fusion.5
  310.1 2.3 add_select_fusion.5
  326.6 2.3 add_select_fusion.5
  332.2 2.3 add_select_fusion.5
  337.7 2.3 add_select_fusion.5
  354.3 2.3 add_select_fusion.5
  359.8 2.3 add_select_fusion.5
  365.3 2.3 add_select_fusion.5
  376.4 2.3 add_select_fusion.5
  409.5 2.3 add_select_fusion.5
  420.6 2.3 add_select_fusion.5
  426.1 2.3 add_select_fusion.5
  431.6 2.3 add_select_fusion.5
  453.8 2.3 add_select_fusion.5
  459.3 2.3 add_select_fusion.5
  464.8 2.3 add_select_fusion.5
  470.3 2.3 add_select_fusion.5
  475.6 102.7 %while.35 = (s32[]{:T(128)}, f32[1024,128]{1,0:T(8,128)S(1)}, bf16[16,512,128]{2,1,0:T(8,128)(2,1)}, bf16[16,512,128]{2,1,0:T(8,128)(2,1)}, bf16[16,512,8]{1,2,0...) while((s32[]{:T(128)}, f32[1024,128]{1,0:T(8,128)S(1)}, ...), condition=%wide.region_9.10_spmd.clone.clone, body=%wide.region_7.9_spmd.clone.sunk.clone | while | flops 270209024 | bytes 4530291 | solution.py:97
  579.5 256.6 %all-reduce.5.cloned.1.call-done = f32[1024,128]{1,0:T(8,128)} async-done(((f32[1024,128]{1,0:T(8,128)}), f32[1024,128]{1,0:T(8,128)}) %all-reduce.5.cloned.1.call-update) | async-done | bytes 524304 | tf_op jit(solution)/shard_map/psum | solution.py:101
  838.0 87.9 %scatter_custom_fusion = f32[2048,128]{1,0:T(8,128)S(1)} fusion(s32[16384]{0:T(1024)S(1)} %bitcast.182, f32[16384,128]{1,0:T(8,128)} %bitcast.17, f32[]{:T(128)} %constant.60.clone.1), kind=kCustom, calls=%fused_computation.33 | custom fusion | flops 2097152 | bytes 1049088 | tf_op jit(solution)/shard_map/scatter-add | solution.py:74
  (472 shorter events, 348.2 us)
Async XLA Ops:
  7.2 97.3 %copy-start = (bf16[1,2048,128]{2,1,0:T(8,128)(2,1)S(1)}, bf16[1,2048,128]{2,1,0:T(8,128)(2,1)}, u32[]{:S(2)}) copy-start(bf16[1,2048,128]{2,1,0:T(8,128)(2,1)} %param.13) | copy-start | bytes 1572868
  52.4 51.7 %all-to-all-start = ((s32[32,1,512]{2,1,0:T(1,128)}), s32[32,1,512]{2,1,0:T(1,128)S(1)}, u32[]{:S(2)}, u32[]{:S(2)}) async-start(s32[32,1,512]{2,1,0:T(1,128)} %compare_select_fusion.2), calls=%async_computation | async-start | bytes 131072 | tf_op jit(solution)/shard_map/all_to_all | solution.py:68
  104.1 57.8 %copy-start.2 = (bf16[16,512,8]{1,2,0:T(8,128)(2,1)}, bf16[16,512,8]{1,2,0:T(8,128)(2,1)S(1)}, u32[]{:S(2)}) copy-start(bf16[16,512,8]{1,2,0:T(8,128)(2,1)S(1)} %get-tuple-element.503) | copy-start | bytes 393220
  169.6 116.9 %all-to-all-start.2 = ((bf16[32,512,128]{2,1,0:T(8,128)(2,1)}), bf16[32,512,128]{2,1,0:T(8,128)(2,1)}, u32[]{:S(2)}, u32[]{:S(2)}) async-start(bf16[32,512,128]{2,1,0:T(8,128)(2,1)} %broadcast_select_fusion.1), calls=%async_computation.2 | async-start | bytes 8388608 | tf_op jit(solution)/shard_map/all_to_all | solution.py:78
  286.5 10.4 %copy-start.3 = (s32[2]{0:T(128)S(1)}, s32[2]{0:T(128)}, u32[]{:S(2)}) copy-start(s32[2]{0:T(128)} %constant.226) | copy-start | bytes 28
  286.5 551.5 %all-to-all-start.1 = ((f32[32,512,128]{2,1,0:T(8,128)}), f32[32,512,128]{2,1,0:T(8,128)}, u32[]{:S(2)}, u32[]{:S(2)}) async-start(f32[32,512,128]{2,1,0:T(8,128)} %broadcast_select_fusion), calls=%async_computation.1 | async-start | bytes 16777216 | tf_op jit(solution)/shard_map/all_to_all | solution.py:67
  296.5 539.6 %all-reduce.5.cloned.1.call-start = ((), (), s32[]{:S(2)}) async-start(), calls=%async_computation.3 | async-start | bytes 1048576 | tf_op jit(solution)/shard_map/psum | solution.py:101
  578.4 0.8 copy-start.1
Sparse Core Ops, SparseCore 0:
  579.3 256.7 all-reduce.4
where the time goes:
time: 940 us; the launch traced here: 934 us
  local copies, waits for them, and re-layouts  298 us (32%)
  waiting for transfers between devices  257 us (27%)
  other arithmetic  255 us (27%)
  matrix products  76.7 us (8%)
  starting transfers between devices  31.4 us (3%)
  between operations  14.2 us (2%)
    psum x1, waiting for transfers between devices, per_device(): summed_terms = lax.psum(weight_term, ('dp', 'space'))  257 us
    gather x192, local copies, waits for them, and re-layouts  135 us
    scatter-add x64, other arithmetic  119 us
    scatter-add x1, other arithmetic, per_device(): summed = jnp.zeros((par_rows, chan_out), jnp.float32).at[recv_parent.resh...  87.9 us
    scatter-add x64, local copies, waits for them, and re-layouts  57.6 us
    gather x1, local copies, waits for them, and re-layouts, per_device(): jnp.take(cotangent, recv_parent, axis=0, mode='fill', fill_value=0)  57.4 us
    dot_general x16, matrix products, backward_block(): jnp.dot(cot, weight_back, preferred_element_type=jnp.float32)  26.9 us
    dot_general x16, matrix products, forward_block(): jnp.dot(rows, weight_cat, preferred_element_type=jnp.float32)  25 us
  transfers between devices with their start and end apart: 4, of which 1 were waited for; matrix products, arithmetic and copies ran while one was open for 46% of the time, Pallas kernels for 0%

commit v1 on v0

--- a/solution.py
+++ b/solution.py
@@ -2,6 +2,7 @@
 import jax.numpy as jnp
 from jax import lax
 from jax.sharding import PartitionSpec as P
+from jax.lax import psum
 
 
 def gather_blocks(rows, starts, capacity):
@@ -98,7 +99,8 @@
         backward_block, start_term, (rows_blocked, onehot_blocked, cot_blocked)
     )
     feature_grad = grad_blocks.reshape(row_count, chan_in)
-    summed_terms = lax.psum(weight_term, ("dp", "space"))
+    piece_next = psum(weight_term, "dp")
+    summed_terms = psum(piece_next, "space")
     total_rows = row_count * space_size * lax.axis_size("dp")
     weight_grad = (summed_terms / jnp.sqrt(jnp.float32(total_rows))).reshape(
         kinds_total, chan_in, chan_out

time: 940 us -> 897 us (0.954)
  waiting for transfers between devices: 257 us -> 219 us
    psum x1 -> x2, waiting for transfers between devices: 257 us -> 219 us  [the longest x1 153 us: per_device(): summed_terms = psum(piece_next, 'space')]
  transfers between devices with their start and end apart: 4 -> 5, of which waited for: 1 -> 2; matrix products, arithmetic and copies ran while one was open for 46% -> 48% of each run, Pallas kernels for 0% -> 0%
where the time goes in v1:
time: 897 us; the launch traced here: 891 us
  local copies, waits for them, and re-layouts  299 us (33%)
  other arithmetic  249 us (28%)
  waiting for transfers between devices  219 us (24%)
  matrix products  76.6 us (9%)
  starting transfers between devices  31.5 us (4%)
  between operations  14.2 us (2%)
    psum x1, waiting for transfers between devices, per_device(): summed_terms = psum(piece_next, 'space')  153 us
    gather x192, local copies, waits for them, and re-layouts  139 us
    scatter-add x64, other arithmetic  112 us
    scatter-add x1, other arithmetic, per_device(): summed = jnp.zeros((par_rows, chan_out), jnp.float32).at[recv_parent.resh...  87.9 us
    psum x1, waiting for transfers between devices, per_device(): piece_next = psum(weight_term, 'dp')  65.4 us
    gather x1, local copies, waits for them, and re-layouts, per_device(): jnp.take(cotangent, recv_parent, axis=0, mode='fill', fill_value=0)  57.4 us
    scatter-add x64, local copies, waits for them, and re-layouts  54.5 us
    dot_general x16, matrix products, backward_block(): jnp.dot(cot, weight_back, preferred_element_type=jnp.float32)  26.9 us
  transfers between devices with their start and end apart: 5, of which 2 were waited for; matrix products, arithmetic and copies ran while one was open for 48% of the time, Pallas kernels for 0%

profile of v1, /device:TPU:2, one launch (start us, length us, event | category | flops | bytes accessed | tf_op | source)
XLA Modules:
  0.0 890.8 jit_solution(13288253710115002579)
XLA Ops:
  9.6 42.1 %while.32 = (s32[]{:T(128)}, s32[8704,1]{0,1:T(1,128)S(1)}, s32[32,2]{0,1:T(2,128)S(1)}, s32[32,512,1]{1,2,0:T(1,128)S(1)}) while((s32[]{:T(128)}, s32[8704,1]{0,1:T(1,128)S(1)}, s32[32,2]{0,1:T(2,128)S(1)}, s32[32,512,1]{1,2,0:T(1,128)S(1)}) %tuple.98), condition=%wide.while_cond.clone, body=%wide.while_body.sunk.clone | while | flops 2 | bytes 4193 | solution.py:12
  52.4 11.5 %all-to-all-start = ((s32[32,1,512]{2,1,0:T(1,128)}), s32[32,1,512]{2,1,0:T(1,128)S(1)}, u32[]{:S(2)}, u32[]{:S(2)}) async-start(s32[32,1,512]{2,1,0:T(1,128)} %compare_select_fusion.2), calls=%async_computation | async-start | bytes 131072 | tf_op jit(solution)/shard_map/all_to_all | solution.py:69
  67.1 36.9 %while.31 = (s32[]{:T(128)}, f32[16,512,128]{2,1,0:T(8,128)}, bf16[16,512,128]{2,1,0:T(8,128)(2,1)}, bf16[128,1024]{0,1:T(8,128)(2,1)S(1)}, bf16[16,512,8]{1,2,0:T(8,128)(2,1)S(1)}) while((s32[]{:T(128)}, f32[16,512,128]{2,1,0:T(8,128)}, bf16[16,512,128]{2,1,0:T(8,128)(2,1)}, bf16[128,1024]{0,1:T(8,128)(2,1)S(1)}, ...), condition=%wide.region_4.5_spmd.clone, body=%wide.region_2.4_spmd.sunk.clone | while | flops 135204864 | bytes 1220689 | solution.py:64
  104.4 57.4 %gather_fusion = bf16[16384,128]{1,0:T(8,128)(2,1)} fusion(bf16[2048,128]{1,0:T(8,128)(2,1)S(1)} %bitcast.167, s32[16384]{0:T(1024)S(1)} %broadcast_clamp_fusion), kind=kCustom, calls=%fused_computation | custom fusion | bytes 8454144 | tf_op jit(solution)/shard_map/jit(_take)/gather | solution.py:78
  161.9 7.7 broadcast_select_fusion.1
  169.6 9.9 %all-to-all-start.2 = ((bf16[32,512,128]{2,1,0:T(8,128)(2,1)}), bf16[32,512,128]{2,1,0:T(8,128)(2,1)}, u32[]{:S(2)}, u32[]{:S(2)}) async-start(bf16[32,512,128]{2,1,0:T(8,128)(2,1)} %broadcast_select_fusion.1), calls=%async_computation.2 | async-start | bytes 8388608 | tf_op jit(solution)/shard_map/all_to_all | solution.py:79
  179.6 3.8 concatenate.12
  183.5 97.5 %while.33 = (s32[]{:T(128)}, f32[8704,128]{1,0:T(8,128)}, s32[32,2]{0,1:T(2,128)S(1)}, f32[32,512,128]{2,1,0:T(8,128)}) while((s32[]{:T(128)}, f32[8704,128]{1,0:T(8,128)}, s32[32,2]{0,1:T(2,128)S(1)}, f32[32,512,128]{2,1,0:T(8,128)}) %tuple.123), condition=%wide.while_cond.1.clone, body=%wide.while_body.1.sunk.clone | while | flops 2 | bytes 524893 | solution.py:12
  184.1 2.4 bitcast_dynamic-update-slice_fusion.14
  187.2 2.4 bitcast_dynamic-update-slice_fusion.14
  190.2 2.4 bitcast_dynamic-update-slice_fusion.14
  193.3 2.4 bitcast_dynamic-update-slice_fusion.14
  196.3 2.4 bitcast_dynamic-update-slice_fusion.14
  199.4 2.4 bitcast_dynamic-update-slice_fusion.14
  202.4 2.4 bitcast_dynamic-update-slice_fusion.14
  205.5 2.4 bitcast_dynamic-update-slice_fusion.14
  208.6 2.4 bitcast_dynamic-update-slice_fusion.14
  211.6 2.4 bitcast_dynamic-update-slice_fusion.14
  214.7 2.4 bitcast_dynamic-update-slice_fusion.14
  217.7 2.4 bitcast_dynamic-update-slice_fusion.14
  220.7 2.4 bitcast_dynamic-update-slice_fusion.14
  223.8 2.4 bitcast_dynamic-update-slice_fusion.14
  226.8 2.4 bitcast_dynamic-update-slice_fusion.14
  229.9 2.4 bitcast_dynamic-update-slice_fusion.14
  232.9 2.4 bitcast_dynamic-update-slice_fusion.14
  236.0 2.4 bitcast_dynamic-update-slice_fusion.14
  239.0 2.4 bitcast_dynamic-update-slice_fusion.14
  242.1 2.4 bitcast_dynamic-update-slice_fusion.14
  245.1 2.4 bitcast_dynamic-update-slice_fusion.14
  248.1 2.4 bitcast_dynamic-update-slice_fusion.14
  251.2 2.4 bitcast_dynamic-update-slice_fusion.14
  254.2 2.4 bitcast_dynamic-update-slice_fusion.14
  257.2 2.4 bitcast_dynamic-update-slice_fusion.14
  260.3 2.4 bitcast_dynamic-update-slice_fusion.14
  263.3 2.4 bitcast_dynamic-update-slice_fusion.14
  266.4 2.4 bitcast_dynamic-update-slice_fusion.14
  269.4 2.4 bitcast_dynamic-update-slice_fusion.14
  272.5 2.4 bitcast_dynamic-update-slice_fusion.14
  275.5 2.4 bitcast_dynamic-update-slice_fusion.14
  278.6 2.4 bitcast_dynamic-update-slice_fusion.14
  280.9 9.9 %broadcast_select_fusion = f32[32,512,128]{2,1,0:T(8,128)} fusion(f32[32,512,128]{2,1,0:T(8,128)} %get-tuple-element.86, pred[32,512]{1,0:T(8,128)(4,1)S(1)} %iota_compare_fusion.2), kind=kLoop, calls=%fused_computation.28 | loop fusion | flops 2097152 | bytes 16793600 | tf_op jit(solution)/shard_map/jit(_where)/select_n | solution.py:66
  290.9 10.0 %all-to-all-start.1 = ((f32[32,512,128]{2,1,0:T(8,128)}), f32[32,512,128]{2,1,0:T(8,128)}, u32[]{:S(2)}, u32[]{:S(2)}) async-start(f32[32,512,128]{2,1,0:T(8,128)} %broadcast_select_fusion), calls=%async_computation.1 | async-start | bytes 16777216 | tf_op jit(solution)/shard_map/all_to_all | solution.py:68
  301.3 167.8 %while.34 = (s32[]{:T(128)}, bf16[8704,128]{1,0:T(8,128)(2,1)S(1)}, s32[32]{0:T(128)S(1)}, bf16[32,512,128]{2,1,0:T(8,128)(2,1)}, s32[2]{0:T(128)S(1)}, /*index=5*/s32[1]{0:T(128)}) while((s32[]{:T(128)}, bf16[8704,128]{1,0:T(8,128)(2,1)S(1)}, s32[32]{0:T(128)S(1)}, bf16[32,512,128]{2,1,0:T(8,128)(2,1)}, s32[2]{0:T(128)S(1)}, ...), condition=%wide.while_cond.2.clone, body=%wide.while_body.2.sunk.clone | while | flops 327691 | bytes 655479 | solution.py:24
  303.2 2.2 add_select_fusion.5
  308.4 2.2 add_select_fusion.5
  313.7 2.2 add_select_fusion.5
  318.9 2.2 add_select_fusion.5
  324.1 2.2 add_select_fusion.5
  329.4 2.2 add_select_fusion.5
  339.8 2.2 add_select_fusion.5
  366.0 2.2 add_select_fusion.5
  376.5 2.2 add_select_fusion.5
  407.8 2.2 add_select_fusion.5
  418.3 2.2 add_select_fusion.5
  423.5 2.2 add_select_fusion.5
  428.8 2.2 add_select_fusion.5
  449.7 2.2 add_select_fusion.5
  454.9 2.2 add_select_fusion.5
  460.2 2.2 add_select_fusion.5
  465.4 2.2 add_select_fusion.5
  470.6 102.7 %while.35 = (s32[]{:T(128)}, f32[1024,128]{1,0:T(8,128)S(1)}, bf16[16,512,128]{2,1,0:T(8,128)(2,1)}, bf16[16,512,128]{2,1,0:T(8,128)(2,1)}, bf16[16,512,8]{1,2,0...) while((s32[]{:T(128)}, f32[1024,128]{1,0:T(8,128)S(1)}, ...), condition=%wide.region_9.10_spmd.clone.clone, body=%wide.region_7.9_spmd.clone.sunk.clone | while | flops 270209024 | bytes 4530291 | solution.py:98
  574.2 65.4 %all-reduce.6.cloned.1.call-done = f32[1024,128]{1,0:T(8,128)} async-done(((f32[1024,128]{1,0:T(8,128)}), f32[1024,128]{1,0:T(8,128)}) %all-reduce.6.cloned.1.call-update) | async-done | bytes 524304 | tf_op jit(solution)/shard_map/psum | solution.py:102
  639.9 153.4 %all-reduce.8.cloned.1.call-done = f32[1024,128]{1,0:T(8,128)} async-done(((f32[1024,128]{1,0:T(8,128)}), f32[1024,128]{1,0:T(8,128)}) %all-reduce.8.cloned.1.call-update) | async-done | bytes 524304 | tf_op jit(solution)/shard_map/psum | solution.py:103
  795.2 87.9 %scatter_custom_fusion = f32[2048,128]{1,0:T(8,128)S(1)} fusion(s32[16384]{0:T(1024)S(1)} %bitcast.182, f32[16384,128]{1,0:T(8,128)} %bitcast.17, f32[]{:T(128)} %constant.60.clone.1), kind=kCustom, calls=%fused_computation.33 | custom fusion | flops 2097152 | bytes 1049088 | tf_op jit(solution)/shard_map/scatter-add | solution.py:75
  (475 shorter events, 344.5 us)
Async XLA Ops:
  7.2 97.3 %copy-start = (bf16[1,2048,128]{2,1,0:T(8,128)(2,1)S(1)}, bf16[1,2048,128]{2,1,0:T(8,128)(2,1)}, u32[]{:S(2)}) copy-start(bf16[1,2048,128]{2,1,0:T(8,128)(2,1)} %param.13) | copy-start | bytes 1572868
  52.4 51.6 %all-to-all-start = ((s32[32,1,512]{2,1,0:T(1,128)}), s32[32,1,512]{2,1,0:T(1,128)S(1)}, u32[]{:S(2)}, u32[]{:S(2)}) async-start(s32[32,1,512]{2,1,0:T(1,128)} %compare_select_fusion.2), calls=%async_computation | async-start | bytes 131072 | tf_op jit(solution)/shard_map/all_to_all | solution.py:69
  104.1 57.8 %copy-start.2 = (bf16[16,512,8]{1,2,0:T(8,128)(2,1)}, bf16[16,512,8]{1,2,0:T(8,128)(2,1)S(1)}, u32[]{:S(2)}) copy-start(bf16[16,512,8]{1,2,0:T(8,128)(2,1)S(1)} %get-tuple-element.507) | copy-start | bytes 393220
  169.6 121.3 %all-to-all-start.2 = ((bf16[32,512,128]{2,1,0:T(8,128)(2,1)}), bf16[32,512,128]{2,1,0:T(8,128)(2,1)}, u32[]{:S(2)}, u32[]{:S(2)}) async-start(bf16[32,512,128]{2,1,0:T(8,128)(2,1)} %broadcast_select_fusion.1), calls=%async_computation.2 | async-start | bytes 8388608 | tf_op jit(solution)/shard_map/all_to_all | solution.py:79
  290.9 10.4 %copy-start.3 = (s32[2]{0:T(128)S(1)}, s32[2]{0:T(128)}, u32[]{:S(2)}) copy-start(s32[2]{0:T(128)} %constant.226) | copy-start | bytes 28
  290.9 504.3 %all-to-all-start.1 = ((f32[32,512,128]{2,1,0:T(8,128)}), f32[32,512,128]{2,1,0:T(8,128)}, u32[]{:S(2)}, u32[]{:S(2)}) async-start(f32[32,512,128]{2,1,0:T(8,128)} %broadcast_select_fusion), calls=%async_computation.1 | async-start | bytes 16777216 | tf_op jit(solution)/shard_map/all_to_all | solution.py:68
  300.9 338.7 %all-reduce.6.cloned.1.call-start = ((), (), s32[]{:S(2)}) async-start(), calls=%async_computation.3 | async-start | bytes 1048576 | tf_op jit(solution)/shard_map/psum | solution.py:102
  573.3 0.8 copy-start.1
  574.1 219.2 %all-reduce.8.cloned.1.call-start = ((), (), s32[]{:S(2)}) async-start(), calls=%async_computation.4 | async-start | bytes 1048576 | tf_op jit(solution)/shard_map/psum | solution.py:103
Sparse Core Ops, SparseCore 0:
  574.2 65.2 all-reduce.5
  643.0 150.3 all-reduce.7
